TPU v7x, 256 devices: a whole 4x4x8 slice. The times are simulated.
256 devices in a mesh: dp: 8 (over x, core), expert: 32 (over y, z).
Axes of the slice: x: 4, y: 4, z: 8, core: 2. Of those that a mesh axis runs over, the one named last changes fastest.
Arguments:
- tokens: bfloat16 [6144, 2048], P(('dp', 'expert')), may hold values from -6 to 6
- out_grad: bfloat16 [6144, 2048], P(('dp', 'expert')), may hold values from -0.59765625 to 0.59765625
- expert_ids: int32 [6144, 8], P(('dp', 'expert')), may hold values from 0 to 31, all different within a row; in each aligned block of 24 rows (0 to 23, 24 to 47, ...) at most 8 rows name the same one
- router_weight: bfloat16 [2048, 32], replicated, may hold values from -0.1875 to 0.1875
- w_gate: bfloat16 [32, 2048, 768], P('expert'), may hold values from -0.125 to 0.125
- w_up: bfloat16 [32, 2048, 768], P('expert'), may hold values from -0.125 to 0.125
- w_down: bfloat16 [32, 768, 2048], P('expert'), may hold values from -0.21875 to 0.21875
Outputs:
- grad_tokens: bfloat16 [6144, 2048], P(('dp', 'expert'))
- grad_router: float32 [2048, 32], replicated
- grad_gate: bfloat16 [32, 2048, 768], P('expert', 'dp')
- grad_up: bfloat16 [32, 2048, 768], P('expert', 'dp')
- grad_down: bfloat16 [32, 768, 2048], P('expert', 'dp')
Inputs may be any that keep to these rules, and one draw needn't show every extreme that they name: `expert_ids`: each row names 8 different experts. Among the 24 tokens of one device (aligned blocks of rows), no expert is named by more than 8 tokens, and in some blocks one expert is named by exactly 8.
All inputs are finite; a program needn't handle non-finite values.
Results may differ from a plain program's by a relative error of at most 0.017.
Values may be sent and summed in bfloat16 or wider, within the bound.
A program may use at most 128 MiB of HBM per device.

v0:
```python
import jax
import jax.numpy as jnp
from jax import lax
from jax.sharding import PartitionSpec as P

PASSES = 3


def expert_rows(rows_in, rows_grad, weight_gate, weight_up, weight_down):
    gate_pre = jnp.dot(rows_in, weight_gate, preferred_element_type=jnp.float32)
    up_pre = jnp.dot(rows_in, weight_up, preferred_element_type=jnp.float32)
    sigmoid_gate = jax.nn.sigmoid(gate_pre)
    activation = gate_pre * sigmoid_gate
    hidden = activation * up_pre
    contract_cols = (((1,), (1,)), ((), ()))
    hidden_grad = lax.dot_general(
        rows_grad, weight_down, contract_cols, preferred_element_type=jnp.float32
    )
    score_grad = jnp.sum(hidden_grad * hidden, axis=1).astype(jnp.bfloat16)
    gate_grad = (
        hidden_grad * up_pre * sigmoid_gate * (1.0 + gate_pre * (1.0 - sigmoid_gate))
    ).astype(jnp.bfloat16)
    up_grad = (hidden_grad * activation).astype(jnp.bfloat16)
    input_grad = lax.dot_general(
        gate_grad, weight_gate, contract_cols, preferred_element_type=jnp.float32
    )
    input_grad = input_grad + lax.dot_general(
        up_grad, weight_up, contract_cols, preferred_element_type=jnp.float32
    )
    return (
        hidden.astype(jnp.bfloat16),
        gate_grad,
        up_grad,
        input_grad.astype(jnp.bfloat16),
        score_grad,
    )


def scaled_rows(gate_values, rows_grad, gate_grad, up_grad):
    gate_scale = gate_values.astype(jnp.float32)[:, None]
    return (
        (gate_scale * rows_grad).astype(jnp.bfloat16),
        (gate_scale * gate_grad).astype(jnp.bfloat16),
        (gate_scale * up_grad).astype(jnp.bfloat16),
    )


def balancer_forward_pass(router_logit_rows):
    expert_density_rows = [jnp.exp(router_logit_rows)]
    division_ratios, column_totals, row_totals = ([], [], [])
    for repeat in range(PASSES):
        column_sum = lax.psum(jnp.sum(expert_density_rows[-1], axis=0), ("dp", "expert"))
        quotient = expert_density_rows[-1] / column_sum
        row_sum = jnp.sum(quotient, axis=1, keepdims=True)
        expert_density_rows.append(quotient / row_sum)
        division_ratios.append(quotient)
        column_totals.append(column_sum)
        row_totals.append(row_sum)
    return (expert_density_rows, division_ratios, column_totals, row_totals)


def balancer_adjoint_pass(
    density_gradient, expert_density_rows, division_ratios, column_totals, row_totals
):
    for repeat in reversed(range(PASSES)):
        density = expert_density_rows[repeat + 1]
        quotient_grad = (
            density_gradient - jnp.sum(density_gradient * density, axis=1, keepdims=True)
        ) / row_totals[repeat]
        shared = lax.psum(
            jnp.sum(quotient_grad * division_ratios[repeat], axis=0), ("dp", "expert")
        )
        density_gradient = (quotient_grad - shared) / column_totals[repeat]
    return density_gradient * expert_density_rows[0]


def column_product(operand_left, operand_right):
    return lax.dot_general(
        operand_left, operand_right, (((0,), (0,)), ((), ())), preferred_element_type=jnp.float32
    )


def per_device(tokens, out_grad, expert_ids, router_weight, w_gate, w_up, w_down):
    tok_rows, model_width = tokens.shape
    expert_blocks = router_weight.shape[1]
    top_picks = expert_ids.shape[1]
    capacity = min(tok_rows, 4 * tok_rows * top_picks // (3 * expert_blocks))
    sources = lax.axis_size("expert")
    slot_total = sources * capacity
    weight_gate, weight_up, weight_down = (w_gate[0], w_up[0], w_down[0])
    ff_width = weight_gate.shape[1]
    highest = lax.Precision.HIGHEST
    router_logit_rows = jnp.dot(tokens, router_weight, preferred_element_type=jnp.float32)
    expert_range = jnp.arange(expert_blocks, dtype=jnp.int32)
    picked = jnp.sum(
        (expert_ids[:, :, None] == expert_range[None, None, :]).astype(jnp.int32), axis=1
    )
    slot_rank = jnp.cumsum(picked, axis=0) - picked
    slot_range = jnp.arange(capacity, dtype=jnp.int32)
    selected = (slot_rank.T[:, None, :] == slot_range[None, :, None]) & (picked.T[:, None, :] > 0)
    select_half = selected.astype(jnp.bfloat16)
    select_full = selected.astype(jnp.float32)
    send_in = jnp.einsum(
        "ect,td->ecd", select_half, tokens, preferred_element_type=jnp.float32
    ).astype(jnp.bfloat16)
    send_grad = jnp.einsum(
        "ect,td->ecd", select_half, out_grad, preferred_element_type=jnp.float32
    ).astype(jnp.bfloat16)
    balancer_state = balancer_forward_pass(router_logit_rows)
    gate_matrix = expert_blocks * balancer_state[0][-1]
    send_gates = jnp.einsum("ect,te->ec", select_full, gate_matrix, precision=highest).astype(
        jnp.bfloat16
    )
    recv_in, recv_grad, recv_gates = (
        lax.all_to_all(send_in, "expert", split_axis=0, concat_axis=0, tiled=True),
        lax.all_to_all(send_grad, "expert", split_axis=0, concat_axis=0, tiled=True),
        lax.all_to_all(send_gates, "expert", split_axis=0, concat_axis=0, tiled=True),
    )
    flat_in = recv_in.reshape(slot_total, model_width)
    flat_grad = recv_grad.reshape(slot_total, model_width)
    hidden, gate_grad, up_grad, input_grad, score_grad = expert_rows(
        flat_in, flat_grad, weight_gate, weight_up, weight_down
    )
    input_slots, score_slots = (input_grad, score_grad)
    back_input, back_score = (
        lax.all_to_all(
            input_slots.reshape(sources, capacity, model_width),
            "expert",
            split_axis=0,
            concat_axis=0,
            tiled=True,
        ),
        lax.all_to_all(
            score_slots.reshape(sources, capacity),
            "expert",
            split_axis=0,
            concat_axis=0,
            tiled=True,
        ),
    )
    gate_values = recv_gates.reshape(slot_total)
    down_scaled, gate_scaled, up_scaled = scaled_rows(gate_values, flat_grad, gate_grad, up_grad)
    paired = jnp.concatenate([gate_scaled, up_scaled], axis=1)
    grad_pair = lax.psum_scatter(
        column_product(flat_in, paired).astype(jnp.bfloat16), "dp", scatter_dimension=0, tiled=True
    ).astype(jnp.float32)
    grad_down = lax.psum_scatter(
        column_product(hidden, down_scaled).astype(jnp.bfloat16),
        "dp",
        scatter_dimension=0,
        tiled=True,
    ).astype(jnp.float32)
    grad_gate = grad_pair[:, :ff_width].astype(jnp.bfloat16)[None]
    grad_up = grad_pair[:, ff_width:].astype(jnp.bfloat16)[None]
    grad_down = grad_down.astype(jnp.bfloat16)[None]
    route_weights = select_full * gate_matrix.T[:, None, :]
    expert_input = jnp.einsum(
        "ect,ecd->td", route_weights, back_input.astype(jnp.float32), precision=highest
    )
    density_gradient = expert_blocks * jnp.einsum(
        "ect,ec->te", select_full, back_score.astype(jnp.float32), precision=highest
    )
    expert_density_rows, division_ratios, column_totals, row_totals = balancer_state
    logit_gradient = balancer_adjoint_pass(
        density_gradient, expert_density_rows, division_ratios, column_totals, row_totals
    ).astype(jnp.bfloat16)
    router_term = lax.dot_general(
        tokens, logit_gradient, (((0,), (0,)), ((), ())), preferred_element_type=jnp.float32
    )
    grad_router = lax.psum(router_term, ("dp", "expert"))
    router_input = lax.dot_general(
        logit_gradient, router_weight, (((1,), (1,)), ((), ())), preferred_element_type=jnp.float32
    )
    grad_tokens = (expert_input + router_input).astype(jnp.bfloat16)
    return (grad_tokens, grad_router, grad_gate, grad_up, grad_down)


def solution(mesh):
    in_specs = (
        P(("dp", "expert"), None),
        P(("dp", "expert"), None),
        P(("dp", "expert"), None),
        P(),
        P("expert", None, None),
        P("expert", None, None),
        P("expert", None, None),
    )
    out_specs = (
        P(("dp", "expert"), None),
        P(),
        P("expert", "dp", None),
        P("expert", "dp", None),
        P("expert", "dp", None),
    )
    return jax.shard_map(
        per_device, mesh=mesh, in_specs=in_specs, out_specs=out_specs, check_vma=False
    )
```

profile of v0, /device:TPU:2, one launch (start us, length us, event | category | flops | bytes accessed | tf_op | source)
XLA Modules:
  0.0 830.9 jit_solution(2231783137656285111)
XLA Ops:
  8.0 0.0 copy-start
  8.0 0.9 copy.34
  9.0 0.1 convert_reduce_fusion
  9.1 1.1 fusion.58
  10.2 78.7 %psum.49 = f32[32]{0:T(128)S(1)} all-reduce(f32[32]{0:T(128)S(1)} %get-tuple-element.16), channel_id=1, replica_groups=mesh['dp'=8,'expert'=32] {'dp','expert'}, use_global_device_ids=true, to_apply=%region_3.4 | all-reduce | flops 32 | bytes 256 | tf_op jit(solution)/shard_map/psum | solution.py:52
  88.9 0.1 fusion.49
  89.0 0.1 fusion.50
  89.2 73.4 %psum.50 = f32[32]{0:T(128)S(1)} all-reduce(f32[32]{0:T(128)S(1)} %fusion.50), channel_id=1, replica_groups=mesh['dp'=8,'expert'=32] {'dp','expert'}, use_global_device_ids=true, to_apply=%region_6.7 | all-reduce | flops 32 | bytes 256 | tf_op jit(solution)/shard_map/psum | solution.py:52
  162.6 0.2 fusion.53
  162.8 0.1 fusion.54
  162.9 74.2 %psum.51 = f32[32]{0:T(128)S(1)} all-reduce(f32[32]{0:T(128)S(1)} %fusion.54), channel_id=1, replica_groups=mesh['dp'=8,'expert'=32] {'dp','expert'}, use_global_device_ids=true, to_apply=%region_9.10 | all-reduce | flops 32 | bytes 256 | tf_op jit(solution)/shard_map/psum | solution.py:52
  237.1 0.2 fusion.55
  237.3 0.1 multiply_bitcast_fusion
  237.5 0.7 copy.40
  238.2 5.9 all-to-all-start.4
  244.1 0.1 copy.35
  244.2 2.3 convolution_convert_fusion.2
  246.5 7.3 all-to-all-done.4
  253.8 4.7 all-to-all-start.1
  258.5 1.4 convolution_convert_fusion.3
  259.9 25.6 %all-to-all-done.1 = bf16[32,8,2048]{2,1,0:T(8,128)(2,1)} async-done(((bf16[32,8,2048]{2,1,0:T(8,128)(2,1)}), bf16[32,8,2048]{2,1,0:T(8,128)(2,1)}, u32[]{:S(2)}, u32[]{:S(2)}) %all-to-all-start.1) | async-done | bytes 1048608 | tf_op jit(solution)/shard_map/all_to_all | solution.py:115
  285.6 5.3 all-to-all-start
  290.9 0.0 reduce-scatter.3.cloned.1.call-start
  290.9 0.1 convert_reduce_fusion.1
  291.0 0.1 reshape.65
  291.1 4.1 fusion.6
  295.1 22.0 %all-to-all-done = bf16[32,8,2048]{2,1,0:T(8,128)(2,1)} async-done(((bf16[32,8,2048]{2,1,0:T(8,128)(2,1)}), bf16[32,8,2048]{2,1,0:T(8,128)(2,1)}, u32[]{:S(2)}, u32[]{:S(2)}) %all-to-all-start) | async-done | bytes 1048608 | tf_op jit(solution)/shard_map/all_to_all | solution.py:116
  317.2 3.3 fusion.8
  320.5 3.6 multiply_convert_fusion.3
  324.1 5.7 convolution_convert_fusion
  329.8 0.0 reduce-scatter.3.cloned.1.call-update
  329.9 0.0 all-reduce.2.cloned.1.call-start
  329.9 0.1 convert_element_type.110
  330.0 14.7 %all_to_all.33 = bf16[32,1,8]{2,1,0:T(2,128)(2,1)S(1)} all-to-all(bf16[32,1,8]{2,1,0:T(2,128)(2,1)S(1)} %convert_element_type.110), channel_id=1, replica_groups=mesh['dp'=8,'expert'=32] {'expert'}, dimensions={0} | all-to-all | bytes 1024 | tf_op jit(solution)/shard_map/all_to_all | solution.py:133
  344.7 0.1 copy.52
  344.8 0.2 fusion.46
  345.0 0.1 multiply_reduce_fusion.5
  345.1 74.4 %psum.52 = f32[32]{0:T(128)S(1)} all-reduce(f32[32]{0:T(128)S(1)} %multiply_reduce_fusion.5), channel_id=1, replica_groups=mesh['dp'=8,'expert'=32] {'dp','expert'}, use_global_device_ids=true, to_apply=%region_14.15 | all-reduce | flops 32 | bytes 256 | tf_op jit(solution)/shard_map/psum | solution.py:70
  419.5 0.2 multiply_reduce_fusion.4
  419.7 0.1 multiply_reduce_fusion.3
  419.9 74.5 %psum.53 = f32[32]{0:T(128)S(1)} all-reduce(f32[32]{0:T(128)S(1)} %get-tuple-element.9), channel_id=1, replica_groups=mesh['dp'=8,'expert'=32] {'dp','expert'}, use_global_device_ids=true, to_apply=%region_17.18 | all-reduce | flops 32 | bytes 256 | tf_op jit(solution)/shard_map/psum | solution.py:70
  494.3 0.2 multiply_reduce_fusion.2
  494.5 0.1 multiply_reduce_fusion.1
  494.6 73.3 %psum.54 = f32[32]{0:T(128)S(1)} all-reduce(f32[32]{0:T(128)S(1)} %multiply_reduce_fusion.1), channel_id=1, replica_groups=mesh['dp'=8,'expert'=32] {'dp','expert'}, use_global_device_ids=true, to_apply=%region_20.21 | all-reduce | flops 32 | bytes 256 | tf_op jit(solution)/shard_map/psum | solution.py:70
  567.9 1.0 convolution_bitcast_fusion
  568.9 0.0 all-reduce.2.cloned.1.call-update
  569.0 0.0 reduce-scatter.5.cloned.1.call-start
  569.1 4.6 convolution_convert_fusion.1
  573.7 0.0 reduce-scatter.5.cloned.1.call-update
  573.7 0.0 copy-start.1
  573.7 0.0 copy-start.4
  573.7 0.9 copy-done.5
  574.7 1.0 fusion
  575.7 0.0 copy-done.1
  575.7 0.0 copy-done.4
  575.8 2.0 fusion.16
  577.8 6.0 all-to-all-start.2
  583.9 0.1 fusion.48
  584.0 28.7 %all-to-all-done.2 = bf16[32,8,2048]{2,1,0:T(8,128)(2,1)} async-done(((bf16[32,8,2048]{2,1,0:T(8,128)(2,1)}), bf16[32,8,2048]{2,1,0:T(8,128)(2,1)}, u32[]{:S(2)}, u32[]{:S(2)}) %all-to-all-start.2) | async-done | bytes 1048608 | tf_op jit(solution)/shard_map/all_to_all | solution.py:126
  612.7 2.4 convolution_bitcast_fusion.1
  615.1 0.9 fusion.19
  616.0 2.0 slice_bitcast_fusion
  618.1 203.8 %all-reduce.2.cloned.1.call-done = f32[2048,32]{0,1:T(8,128)} async-done(((f32[2048,32]{0,1:T(8,128)}), f32[2048,32]{0,1:T(8,128)}) %all-reduce.2.cloned.1.call-update) | async-done | bytes 262160 | tf_op jit(solution)/shard_map/psum | solution.py:170
  821.8 1.7 copy.56
  (63 shorter events, 0.3 us)
Async XLA Ops:
  8.0 312.5 %copy-start = (bf16[1,2048,768]{2,1,0:T(8,128)(2,1)S(1)}, bf16[1,2048,768]{2,1,0:T(8,128)(2,1)}, u32[]{:S(2)}) copy-start(bf16[1,2048,768]{2,1,0:T(8,128)(2,1)} %param.11) | copy-start | bytes 9437188
  8.0 250.5 %copy-start.12 = (bf16[24,2048]{1,0:T(8,128)(2,1)S(1)}, bf16[24,2048]{1,0:T(8,128)(2,1)}, u32[]{:S(2)}) copy-start(bf16[24,2048]{1,0:T(8,128)(2,1)} %param.8) | copy-start | bytes 294916
  89.0 478.9 %copy-start.10 = (f32[24]{0:T(128)}, f32[24]{0:T(128)S(1)}, u32[]{:S(2)}) copy-start(f32[24]{0:T(128)S(1)} %fusion.49) | copy-start | bytes 292
  89.2 255.6 %copy-start.8 = (s32[32,24]{0,1:T(8,128)}, s32[32,24]{0,1:T(8,128)S(1)}, u32[]{:S(2)}) copy-start(s32[32,24]{0,1:T(8,128)S(1)} %subtract_bitcast_fusion) | copy-start | bytes 9220
  162.6 405.3 %copy-start.13 = (f32[32]{0:T(128)}, f32[32]{0:T(128)S(1)}, u32[]{:S(2)}) copy-start(f32[32]{0:T(128)S(1)} %psum.50) | copy-start | bytes 388
  162.8 256.9 %copy-start.17 = (f32[24]{0:T(128)}, f32[24]{0:T(128)S(1)}, u32[]{:S(2)}) copy-start(f32[24]{0:T(128)S(1)} %fusion.53) | copy-start | bytes 292
  162.9 181.9 %copy-start.15 = (pred[32,24]{0,1:T(8,128)(4,1)}, pred[32,24]{0,1:T(8,128)(4,1)S(1)}, u32[]{:S(2)}) copy-start(pred[32,24]{0,1:T(8,128)(4,1)S(1)} %compare_bitcast_fusion) | copy-start | bytes 2308
  237.1 182.6 %copy-start.19 = (f32[32]{0:T(128)}, f32[32]{0:T(128)S(1)}, u32[]{:S(2)}) copy-start(f32[32]{0:T(128)S(1)} %psum.51) | copy-start | bytes 388
  237.3 182.4 %copy-start.21 = (f32[24]{0:T(128)}, f32[24]{0:T(128)S(1)}, u32[]{:S(2)}) copy-start(f32[24]{0:T(128)S(1)} %fusion.55) | copy-start | bytes 292
  238.2 15.6 %all-to-all-start.4 = ((bf16[32,1,8]{2,1,0:T(2,128)(2,1)}), bf16[32,1,8]{2,1,0:T(2,128)(2,1)S(1)}, u32[]{:S(2)}, u32[]{:S(2)}) async-start(bf16[32,1,8]{2,1,0:T(2,128)(2,1)} %copy.40), calls=%async_computation.4 | async-start | bytes 32768 | tf_op jit(solution)/shard_map/all_to_all | solution.py:117
  253.8 31.8 %all-to-all-start.1 = ((bf16[32,8,2048]{2,1,0:T(8,128)(2,1)}), bf16[32,8,2048]{2,1,0:T(8,128)(2,1)}, u32[]{:S(2)}, u32[]{:S(2)}) async-start(bf16[32,8,2048]{2,1,0:T(8,128)(2,1)} %convolution_convert_fusion.2), calls=%async_computation.1 | async-start | bytes 2097152 | tf_op jit(solution)/shard_map/all_to_all | solution.py:115
  285.6 31.6 %all-to-all-start = ((bf16[32,8,2048]{2,1,0:T(8,128)(2,1)}), bf16[32,8,2048]{2,1,0:T(8,128)(2,1)}, u32[]{:S(2)}, u32[]{:S(2)}) async-start(bf16[32,8,2048]{2,1,0:T(8,128)(2,1)} %convolution_convert_fusion.3), calls=%async_computation | async-start | bytes 2097152 | tf_op jit(solution)/shard_map/all_to_all | solution.py:116
  290.9 325.1 %reduce-scatter.3.cloned.1.call-start = ((), (), s32[]{:S(2)}) async-start(), calls=%async_computation.8 | async-start | bytes 7077888 | tf_op jit(solution)/shard_map/reduce_scatter | solution.py:144
  317.2 3.3 copy-start.29
  329.8 238.1 %copy-start.2 = (bf16[24,2048]{1,0:T(8,128)(2,1)S(1)}, bf16[24,2048]{1,0:T(8,128)(2,1)}, u32[]{:S(2)}) copy-start(bf16[24,2048]{1,0:T(8,128)(2,1)} %param.7) | copy-start | bytes 294916
  329.9 492.0 %all-reduce.2.cloned.1.call-start = ((), (), s32[]{:S(2)}) async-start(), calls=%async_computation.7 | async-start | bytes 524288 | tf_op jit(solution)/shard_map/psum | solution.py:170
  419.9 149.2 %copy-start.6 = (f32[24,32]{1,0:T(8,128)}, f32[24,32]{1,0:T(8,128)S(1)}, u32[]{:S(2)}) copy-start(f32[24,32]{1,0:T(8,128)S(1)} %get-tuple-element.10) | copy-start | bytes 9220
  494.3 74.7 %copy-start.23 = (f32[32]{0:T(128)}, f32[32]{0:T(128)S(1)}, u32[]{:S(2)}) copy-start(f32[32]{0:T(128)S(1)} %psum.53) | copy-start | bytes 388
  494.5 74.5 %copy-start.25 = (f32[24]{0:T(128)}, f32[24]{0:T(128)S(1)}, u32[]{:S(2)}) copy-start(f32[24]{0:T(128)S(1)} %multiply_reduce_fusion.2) | copy-start | bytes 292
  567.9 1.1 copy-start.27
  569.0 252.9 %reduce-scatter.5.cloned.1.call-start = ((), (), s32[]{:S(2)}) async-start(), calls=%async_computation.9 | async-start | bytes 3538944 | tf_op jit(solution)/shard_map/reduce_scatter | solution.py:147
  573.7 1.0 copy-start.5
  573.7 2.0 copy-start.1
  573.7 2.0 copy-start.4
  575.7 8.1 copy-start.11
  575.7 8.1 copy-start.14
  575.7 8.1 copy-start.18
  575.7 8.1 copy-start.20
  575.7 8.1 copy-start.22
  575.7 36.9 %copy-start.9 = (s32[32,24]{0,1:T(8,128)S(1)}, s32[32,24]{0,1:T(8,128)}, u32[]{:S(2)}) copy-start(s32[32,24]{0,1:T(8,128)} %copy-done.8) | copy-start | bytes 9220
  575.8 36.9 %copy-start.16 = (pred[32,24]{0,1:T(8,128)(4,1)S(1)}, pred[32,24]{0,1:T(8,128)(4,1)}, u32[]{:S(2)}) copy-start(pred[32,24]{0,1:T(8,128)(4,1)} %copy-done.15) | copy-start | bytes 2308
  577.8 37.3 %copy-start.3 = (bf16[2048,32]{0,1:T(8,128)(2,1)S(1)}, bf16[2048,32]{0,1:T(8,128)(2,1)}, u32[]{:S(2)}) copy-start(bf16[2048,32]{0,1:T(8,128)(2,1)} %param.10) | copy-start | bytes 393220
  577.8 37.3 %copy-start.7 = (f32[24,32]{1,0:T(8,128)S(1)}, f32[24,32]{1,0:T(8,128)}, u32[]{:S(2)}) copy-start(f32[24,32]{1,0:T(8,128)} %copy-done.6) | copy-start | bytes 9220
  577.8 37.3 %copy-start.24 = (f32[32]{0:T(128)S(1)}, f32[32]{0:T(128)}, u32[]{:S(2)}) copy-start(f32[32]{0:T(128)} %copy-done.23) | copy-start | bytes 388
  577.8 37.3 %copy-start.26 = (f32[24]{0:T(128)S(1)}, f32[24]{0:T(128)}, u32[]{:S(2)}) copy-start(f32[24]{0:T(128)} %copy-done.25) | copy-start | bytes 292
  577.8 37.3 %copy-start.28 = (f32[32]{0:T(128)S(1)}, f32[32]{0:T(128)}, u32[]{:S(2)}) copy-start(f32[32]{0:T(128)} %copy-done.27) | copy-start | bytes 388
  577.8 34.9 %all-to-all-start.2 = ((bf16[32,8,2048]{2,1,0:T(8,128)(2,1)}), bf16[32,8,2048]{2,1,0:T(8,128)(2,1)}, u32[]{:S(2)}, u32[]{:S(2)}) async-start(bf16[32,8,2048]{2,1,0:T(8,128)(2,1)} %fusion.16), calls=%async_computation.2 | async-start | bytes 2097152 | tf_op jit(solution)/shard_map/all_to_all | solution.py:126
Sparse Core Ops, SparseCore 0:
  330.0 40.7 reduce-scatter.2
  573.8 31.8 reduce-scatter.4
Sparse Core Ops, SparseCore 1:
  569.0 252.7 all-reduce.1
where the time goes:
time: 832 us; the launch traced here: 831 us
  blocking collectives  463 us (56%)
  waiting for transfers between devices  287 us (34%)
  matrix products  33.5 us (4%)
  starting transfers between devices  22 us (3%)
  between operations  15.9 us (2%)
    psum x3, blocking collectives, balancer_forward_pass(): lax.psum(jnp.sum(expert_density_rows[-1], axis=0), ('dp', 'expert'))  226 us
    psum x3, blocking collectives, balancer_adjoint_pass(): lax.psum(jnp.sum(quotient_grad * division_ratios[repeat], axis=0), ('dp',...  222 us
    psum x1, waiting for transfers between devices, per_device(): grad_router = lax.psum(router_term, ('dp', 'expert'))  204 us
    all_to_all x1, waiting for transfers between devices, per_device(): lax.all_to_all(input_slots.reshape(sources, capacity, model_width), 'expe...  28.7 us
    all_to_all x1, waiting for transfers between devices, per_device(): lax.all_to_all(send_in, 'expert', split_axis=0, concat_axis=0, tiled=True)  25.6 us
    all_to_all x1, waiting for transfers between devices, per_device(): lax.all_to_all(send_grad, 'expert', split_axis=0, concat_axis=0, tiled=True)  22 us
  transfers between devices with their start and end apart: 7, of which 5 were waited for; matrix products, arithmetic and copies ran while one was open for 3% of the time, Pallas kernels for 0%

commit v1 on v0

--- a/solution.py
+++ b/solution.py
@@ -167,7 +167,7 @@
     router_term = lax.dot_general(
         tokens, logit_gradient, (((0,), (0,)), ((), ())), preferred_element_type=jnp.float32
     )
-    grad_router = lax.psum(router_term, ("dp", "expert"))
+    grad_router = lax.psum(lax.psum(router_term, "dp"), "expert")
     router_input = lax.dot_general(
         logit_gradient, router_weight, (((1,), (1,)), ((), ())), preferred_element_type=jnp.float32
     )

time: 832 us -> 868 us (1.043)
  waiting for transfers between devices: 287 us -> 317 us
    reduce_scatter x1, waiting for transfers between devices: 0.01 us -> 35.1 us  [per_device(): lax.psum_scatter(column_product(hidden, down_scaled).astype(jnp.bfloat16)...]
    psum x1 -> x2, waiting for transfers between devices: 204 us -> 201 us  [per_device(): grad_router = lax.psum(lax.psum(router_term, 'dp'), 'expert')]
  transfers between devices with their start and end apart: 7 -> 8, of which waited for: 5 -> 7; matrix products, arithmetic and copies ran while one was open for 3% -> 3% of each run, Pallas kernels for 0% -> 0%
where the time goes in v1:
time: 868 us; the launch traced here: 863 us
  blocking collectives  462 us (53%)
  waiting for transfers between devices  317 us (37%)
  matrix products  34.1 us (4%)
  starting transfers between devices  26.3 us (3%)
  between operations  14.2 us (2%)
    psum x3, blocking collectives, balancer_forward_pass(): lax.psum(jnp.sum(expert_density_rows[-1], axis=0), ('dp', 'expert'))  226 us
    psum x3, blocking collectives, balancer_adjoint_pass(): lax.psum(jnp.sum(quotient_grad * division_ratios[repeat], axis=0), ('dp',...  221 us
    psum x2, waiting for transfers between devices, per_device(): grad_router = lax.psum(lax.psum(router_term, 'dp'), 'expert')  201 us
    reduce_scatter x1, waiting for transfers between devices, per_device(): lax.psum_scatter(column_product(hidden, down_scaled).astype(jnp.bfloat16)...  35.1 us
    all_to_all x1, waiting for transfers between devices, per_device(): lax.all_to_all(input_slots.reshape(sources, capacity, model_width), 'expe...  26.4 us
    all_to_all x1, waiting for transfers between devices, per_device(): lax.all_to_all(send_in, 'expert', split_axis=0, concat_axis=0, tiled=True)  25.5 us
    all_to_all x1, waiting for transfers between devices, per_device(): lax.all_to_all(send_grad, 'expert', split_axis=0, concat_axis=0, tiled=True)  22 us
  transfers between devices with their start and end apart: 8, of which 7 were waited for; matrix products, arithmetic and copies ran while one was open for 3% of the time, Pallas kernels for 0%

profile of v1, /device:TPU:2, one launch (start us, length us, event | category | flops | bytes accessed | tf_op | source)
XLA Modules:
  0.0 862.9 jit_solution(16193722566653267792)
XLA Ops:
  7.2 0.9 copy.34
  8.1 0.1 convert_reduce_fusion
  8.2 1.1 fusion.58
  9.4 78.7 %psum.56 = f32[32]{0:T(128)S(1)} all-reduce(f32[32]{0:T(128)S(1)} %get-tuple-element.16), channel_id=1, replica_groups=mesh['dp'=8,'expert'=32] {'dp','expert'}, use_global_device_ids=true, to_apply=%region_3.4 | all-reduce | flops 32 | bytes 256 | tf_op jit(solution)/shard_map/psum | solution.py:52
  88.1 0.1 fusion.49
  88.2 0.1 fusion.50
  88.3 73.4 %psum.57 = f32[32]{0:T(128)S(1)} all-reduce(f32[32]{0:T(128)S(1)} %fusion.50), channel_id=1, replica_groups=mesh['dp'=8,'expert'=32] {'dp','expert'}, use_global_device_ids=true, to_apply=%region_6.7 | all-reduce | flops 32 | bytes 256 | tf_op jit(solution)/shard_map/psum | solution.py:52
  161.7 0.2 fusion.53
  161.9 0.1 fusion.54
  162.0 74.2 %psum.58 = f32[32]{0:T(128)S(1)} all-reduce(f32[32]{0:T(128)S(1)} %fusion.54), channel_id=1, replica_groups=mesh['dp'=8,'expert'=32] {'dp','expert'}, use_global_device_ids=true, to_apply=%region_9.10 | all-reduce | flops 32 | bytes 256 | tf_op jit(solution)/shard_map/psum | solution.py:52
  236.2 0.2 fusion.55
  236.4 0.1 multiply_bitcast_fusion
  236.6 0.7 copy.40
  237.3 5.9 all-to-all-start.4
  243.2 0.1 copy.35
  243.3 2.3 convolution_convert_fusion.2
  245.6 7.3 all-to-all-done.4
  252.9 4.7 all-to-all-start.1
  257.6 1.5 convolution_convert_fusion.3
  259.1 25.5 %all-to-all-done.1 = bf16[32,8,2048]{2,1,0:T(8,128)(2,1)} async-done(((bf16[32,8,2048]{2,1,0:T(8,128)(2,1)}), bf16[32,8,2048]{2,1,0:T(8,128)(2,1)}, u32[]{:S(2)}, u32[]{:S(2)}) %all-to-all-start.1) | async-done | bytes 1048608 | tf_op jit(solution)/shard_map/all_to_all | solution.py:115
  284.6 5.3 all-to-all-start
  290.0 0.0 all-reduce.3.cloned.1.call-start
  290.0 0.1 convert_reduce_fusion.1
  290.1 0.1 reshape.65
  290.1 4.1 fusion.6
  294.2 22.0 %all-to-all-done = bf16[32,8,2048]{2,1,0:T(8,128)(2,1)} async-done(((bf16[32,8,2048]{2,1,0:T(8,128)(2,1)}), bf16[32,8,2048]{2,1,0:T(8,128)(2,1)}, u32[]{:S(2)}, u32[]{:S(2)}) %all-to-all-start) | async-done | bytes 1048608 | tf_op jit(solution)/shard_map/all_to_all | solution.py:116
  316.3 3.3 fusion.8
  319.6 3.9 multiply_convert_fusion.3
  323.5 0.1 convert_element_type.110
  323.6 14.7 %all_to_all.33 = bf16[32,1,8]{2,1,0:T(2,128)(2,1)S(1)} all-to-all(bf16[32,1,8]{2,1,0:T(2,128)(2,1)S(1)} %convert_element_type.110), channel_id=1, replica_groups=mesh['dp'=8,'expert'=32] {'expert'}, dimensions={0} | all-to-all | bytes 1024 | tf_op jit(solution)/shard_map/all_to_all | solution.py:133
  338.3 0.1 copy.52
  338.4 0.2 fusion.46
  338.6 0.1 multiply_reduce_fusion.5
  338.7 73.8 %psum.59 = f32[32]{0:T(128)S(1)} all-reduce(f32[32]{0:T(128)S(1)} %multiply_reduce_fusion.5), channel_id=1, replica_groups=mesh['dp'=8,'expert'=32] {'dp','expert'}, use_global_device_ids=true, to_apply=%region_14.15 | all-reduce | flops 32 | bytes 256 | tf_op jit(solution)/shard_map/psum | solution.py:70
  412.5 0.2 multiply_reduce_fusion.4
  412.7 0.1 multiply_reduce_fusion.3
  412.8 74.2 %psum.60 = f32[32]{0:T(128)S(1)} all-reduce(f32[32]{0:T(128)S(1)} %get-tuple-element.9), channel_id=1, replica_groups=mesh['dp'=8,'expert'=32] {'dp','expert'}, use_global_device_ids=true, to_apply=%region_17.18 | all-reduce | flops 32 | bytes 256 | tf_op jit(solution)/shard_map/psum | solution.py:70
  487.0 0.2 multiply_reduce_fusion.2
  487.2 0.1 multiply_reduce_fusion.1
  487.3 73.3 %psum.61 = f32[32]{0:T(128)S(1)} all-reduce(f32[32]{0:T(128)S(1)} %multiply_reduce_fusion.1), channel_id=1, replica_groups=mesh['dp'=8,'expert'=32] {'dp','expert'}, use_global_device_ids=true, to_apply=%region_20.21 | all-reduce | flops 32 | bytes 256 | tf_op jit(solution)/shard_map/psum | solution.py:70
  560.6 1.0 convolution_bitcast_fusion
  561.6 0.0 all-reduce.3.cloned.1.call-update
  561.7 0.2 reduce-scatter.3.cloned.1.call-start
  561.9 5.9 convolution_convert_fusion
  567.8 0.0 reduce-scatter.3.cloned.1.call-update
  567.8 0.0 all-reduce.5.cloned.1.call-start
  567.9 53.0 %all-reduce.3.cloned.1.call-done = f32[2048,32]{0,1:T(8,128)} async-done(((f32[2048,32]{0,1:T(8,128)}), f32[2048,32]{0,1:T(8,128)}) %all-reduce.3.cloned.1.call-update) | async-done | bytes 262160 | tf_op jit(solution)/shard_map/psum | solution.py:170
  620.9 0.0 all-reduce.5.cloned.1.call-update
  621.0 0.0 reduce-scatter.5.cloned.1.call-start
  621.0 4.6 convolution_convert_fusion.1
  625.6 0.0 reduce-scatter.5.cloned.1.call-update
  625.6 0.9 copy-done.5
  626.6 1.0 fusion
  627.6 0.0 copy-done.4
  627.7 2.0 fusion.16
  629.7 10.1 %all-to-all-start.2 = ((bf16[32,8,2048]{2,1,0:T(8,128)(2,1)}), bf16[32,8,2048]{2,1,0:T(8,128)(2,1)}, u32[]{:S(2)}, u32[]{:S(2)}) async-start(bf16[32,8,2048]{2,1,0:T(8,128)(2,1)} %fusion.16), calls=%async_computation.2 | async-start | bytes 2097152 | tf_op jit(solution)/shard_map/all_to_all | solution.py:126
  639.9 0.1 fusion.48
  640.0 26.4 %all-to-all-done.2 = bf16[32,8,2048]{2,1,0:T(8,128)(2,1)} async-done(((bf16[32,8,2048]{2,1,0:T(8,128)(2,1)}), bf16[32,8,2048]{2,1,0:T(8,128)(2,1)}, u32[]{:S(2)}, u32[]{:S(2)}) %all-to-all-start.2) | async-done | bytes 1048608 | tf_op jit(solution)/shard_map/all_to_all | solution.py:126
  666.4 2.4 convolution_bitcast_fusion.1
  668.9 0.9 fusion.19
  669.7 2.0 slice_bitcast_fusion
  671.8 147.8 %all-reduce.5.cloned.1.call-done = f32[2048,32]{0,1:T(8,128)} async-done(((f32[2048,32]{0,1:T(8,128)}), f32[2048,32]{0,1:T(8,128)}) %all-reduce.5.cloned.1.call-update) | async-done | bytes 262160 | tf_op jit(solution)/shard_map/psum | solution.py:170
  819.6 35.1 %reduce-scatter.5.cloned.1.call-done = bf16[96,2048]{1,0:T(8,128)(2,1)} async-done(((bf16[768,2048]{1,0:T(8,128)(2,1)}), bf16[96,2048]{1,0:T(8,128)(2,1)}) %reduce-scatter.5.cloned.1.call-update) | async-done | bytes 393232 | tf_op jit(solution)/shard_map/reduce_scatter | solution.py:147
  854.7 1.7 copy.57
  (66 shorter events, 0.3 us)
Async XLA Ops:
  7.2 312.4 %copy-start = (bf16[1,2048,768]{2,1,0:T(8,128)(2,1)S(1)}, bf16[1,2048,768]{2,1,0:T(8,128)(2,1)}, u32[]{:S(2)}) copy-start(bf16[1,2048,768]{2,1,0:T(8,128)(2,1)} %param.11) | copy-start | bytes 9437188
  7.2 250.4 %copy-start.12 = (bf16[24,2048]{1,0:T(8,128)(2,1)S(1)}, bf16[24,2048]{1,0:T(8,128)(2,1)}, u32[]{:S(2)}) copy-start(bf16[24,2048]{1,0:T(8,128)(2,1)} %param.8) | copy-start | bytes 294916
  88.2 472.5 %copy-start.10 = (f32[24]{0:T(128)}, f32[24]{0:T(128)S(1)}, u32[]{:S(2)}) copy-start(f32[24]{0:T(128)S(1)} %fusion.49) | copy-start | bytes 292
  88.3 250.0 %copy-start.8 = (s32[32,24]{0,1:T(8,128)}, s32[32,24]{0,1:T(8,128)S(1)}, u32[]{:S(2)}) copy-start(s32[32,24]{0,1:T(8,128)S(1)} %subtract_bitcast_fusion) | copy-start | bytes 9220
  161.7 398.9 %copy-start.13 = (f32[32]{0:T(128)}, f32[32]{0:T(128)S(1)}, u32[]{:S(2)}) copy-start(f32[32]{0:T(128)S(1)} %psum.57) | copy-start | bytes 388
  161.9 250.7 %copy-start.17 = (f32[24]{0:T(128)}, f32[24]{0:T(128)S(1)}, u32[]{:S(2)}) copy-start(f32[24]{0:T(128)S(1)} %fusion.53) | copy-start | bytes 292
  162.0 176.3 %copy-start.15 = (pred[32,24]{0,1:T(8,128)(4,1)}, pred[32,24]{0,1:T(8,128)(4,1)S(1)}, u32[]{:S(2)}) copy-start(pred[32,24]{0,1:T(8,128)(4,1)S(1)} %compare_bitcast_fusion) | copy-start | bytes 2308
  236.2 176.4 %copy-start.19 = (f32[32]{0:T(128)}, f32[32]{0:T(128)S(1)}, u32[]{:S(2)}) copy-start(f32[32]{0:T(128)S(1)} %psum.58) | copy-start | bytes 388
  236.4 176.2 %copy-start.21 = (f32[24]{0:T(128)}, f32[24]{0:T(128)S(1)}, u32[]{:S(2)}) copy-start(f32[24]{0:T(128)S(1)} %fusion.55) | copy-start | bytes 292
  237.3 15.6 %all-to-all-start.4 = ((bf16[32,1,8]{2,1,0:T(2,128)(2,1)}), bf16[32,1,8]{2,1,0:T(2,128)(2,1)S(1)}, u32[]{:S(2)}, u32[]{:S(2)}) async-start(bf16[32,1,8]{2,1,0:T(2,128)(2,1)} %copy.40), calls=%async_computation.4 | async-start | bytes 32768 | tf_op jit(solution)/shard_map/all_to_all | solution.py:117
  252.9 31.7 %all-to-all-start.1 = ((bf16[32,8,2048]{2,1,0:T(8,128)(2,1)}), bf16[32,8,2048]{2,1,0:T(8,128)(2,1)}, u32[]{:S(2)}, u32[]{:S(2)}) async-start(bf16[32,8,2048]{2,1,0:T(8,128)(2,1)} %convolution_convert_fusion.2), calls=%async_computation.1 | async-start | bytes 2097152 | tf_op jit(solution)/shard_map/all_to_all | solution.py:115
  284.6 31.6 %all-to-all-start = ((bf16[32,8,2048]{2,1,0:T(8,128)(2,1)}), bf16[32,8,2048]{2,1,0:T(8,128)(2,1)}, u32[]{:S(2)}, u32[]{:S(2)}) async-start(bf16[32,8,2048]{2,1,0:T(8,128)(2,1)} %convolution_convert_fusion.3), calls=%async_computation | async-start | bytes 2097152 | tf_op jit(solution)/shard_map/all_to_all | solution.py:116
  290.0 331.0 %all-reduce.3.cloned.1.call-start = ((), (), s32[]{:S(2)}) async-start(), calls=%async_computation.7 | async-start | bytes 524288 | tf_op jit(solution)/shard_map/psum | solution.py:170
  316.2 3.3 copy-start.29
  319.6 241.1 %copy-start.2 = (bf16[24,2048]{1,0:T(8,128)(2,1)S(1)}, bf16[24,2048]{1,0:T(8,128)(2,1)}, u32[]{:S(2)}) copy-start(bf16[24,2048]{1,0:T(8,128)(2,1)} %param.7) | copy-start | bytes 294916
  412.8 155.0 %copy-start.6 = (f32[24,32]{1,0:T(8,128)}, f32[24,32]{1,0:T(8,128)S(1)}, u32[]{:S(2)}) copy-start(f32[24,32]{1,0:T(8,128)S(1)} %get-tuple-element.10) | copy-start | bytes 9220
  487.0 80.8 %copy-start.23 = (f32[32]{0:T(128)}, f32[32]{0:T(128)S(1)}, u32[]{:S(2)}) copy-start(f32[32]{0:T(128)S(1)} %psum.60) | copy-start | bytes 388
  487.2 80.6 %copy-start.25 = (f32[24]{0:T(128)}, f32[24]{0:T(128)S(1)}, u32[]{:S(2)}) copy-start(f32[24]{0:T(128)S(1)} %multiply_reduce_fusion.2) | copy-start | bytes 292
  560.6 7.2 copy-start.27
  561.7 108.1 %reduce-scatter.3.cloned.1.call-start = ((), (), s32[]{:S(2)}) async-start(), calls=%async_computation.9 | async-start | bytes 7077888 | tf_op jit(solution)/shard_map/reduce_scatter | solution.py:144
  567.8 251.7 %all-reduce.5.cloned.1.call-start = ((), (), s32[]{:S(2)}) async-start(), calls=%async_computation.8 | async-start | bytes 524288 | tf_op jit(solution)/shard_map/psum | solution.py:170
  621.0 233.7 %reduce-scatter.5.cloned.1.call-start = ((), (), s32[]{:S(2)}) async-start(), calls=%async_computation.10 | async-start | bytes 3538944 | tf_op jit(solution)/shard_map/reduce_scatter | solution.py:147
  625.6 1.0 copy-start.5
  625.6 2.0 copy-start.1
  625.6 2.0 copy-start.4
  627.7 12.2 %copy-start.11 = (f32[24]{0:T(128)S(1)}, f32[24]{0:T(128)}, u32[]{:S(2)}) copy-start(f32[24]{0:T(128)} %copy-done.10) | copy-start | bytes 292
  627.7 12.2 %copy-start.14 = (f32[32]{0:T(128)S(1)}, f32[32]{0:T(128)}, u32[]{:S(2)}) copy-start(f32[32]{0:T(128)} %copy-done.13) | copy-start | bytes 388
  627.7 12.2 %copy-start.18 = (f32[24]{0:T(128)S(1)}, f32[24]{0:T(128)}, u32[]{:S(2)}) copy-start(f32[24]{0:T(128)} %copy-done.17) | copy-start | bytes 292
  627.7 12.2 %copy-start.20 = (f32[32]{0:T(128)S(1)}, f32[32]{0:T(128)}, u32[]{:S(2)}) copy-start(f32[32]{0:T(128)} %copy-done.19) | copy-start | bytes 388
  627.7 12.2 %copy-start.22 = (f32[24]{0:T(128)S(1)}, f32[24]{0:T(128)}, u32[]{:S(2)}) copy-start(f32[24]{0:T(128)} %copy-done.21) | copy-start | bytes 292
  627.7 38.7 %copy-start.9 = (s32[32,24]{0,1:T(8,128)S(1)}, s32[32,24]{0,1:T(8,128)}, u32[]{:S(2)}) copy-start(s32[32,24]{0,1:T(8,128)} %copy-done.8) | copy-start | bytes 9220
  627.7 38.7 %copy-start.16 = (pred[32,24]{0,1:T(8,128)(4,1)S(1)}, pred[32,24]{0,1:T(8,128)(4,1)}, u32[]{:S(2)}) copy-start(pred[32,24]{0,1:T(8,128)(4,1)} %copy-done.15) | copy-start | bytes 2308
  629.7 39.1 %copy-start.3 = (bf16[2048,32]{0,1:T(8,128)(2,1)S(1)}, bf16[2048,32]{0,1:T(8,128)(2,1)}, u32[]{:S(2)}) copy-start(bf16[2048,32]{0,1:T(8,128)(2,1)} %param.10) | copy-start | bytes 393220
  629.7 39.1 %copy-start.7 = (f32[24,32]{1,0:T(8,128)S(1)}, f32[24,32]{1,0:T(8,128)}, u32[]{:S(2)}) copy-start(f32[24,32]{1,0:T(8,128)} %copy-done.6) | copy-start | bytes 9220
  629.7 39.1 %copy-start.24 = (f32[32]{0:T(128)S(1)}, f32[32]{0:T(128)}, u32[]{:S(2)}) copy-start(f32[32]{0:T(128)} %copy-done.23) | copy-start | bytes 388
  629.7 39.1 %copy-start.26 = (f32[24]{0:T(128)S(1)}, f32[24]{0:T(128)}, u32[]{:S(2)}) copy-start(f32[24]{0:T(128)} %copy-done.25) | copy-start | bytes 292
  629.7 39.1 %copy-start.28 = (f32[32]{0:T(128)S(1)}, f32[32]{0:T(128)}, u32[]{:S(2)}) copy-start(f32[32]{0:T(128)} %copy-done.27) | copy-start | bytes 388
  629.7 36.7 %all-to-all-start.2 = ((bf16[32,8,2048]{2,1,0:T(8,128)(2,1)}), bf16[32,8,2048]{2,1,0:T(8,128)(2,1)}, u32[]{:S(2)}, u32[]{:S(2)}) async-start(bf16[32,8,2048]{2,1,0:T(8,128)(2,1)} %fusion.16), calls=%async_computation.2 | async-start | bytes 2097152 | tf_op jit(solution)/shard_map/all_to_all | solution.py:126
Sparse Core Ops, SparseCore 0:
  561.8 59.0 all-reduce.2
  623.5 44.3 reduce-scatter.2
  671.4 148.1 all-reduce.4
  822.6 32.0 reduce-scatter.4
